TPU v7x, 512 devices: a whole 4x4x16 slice. The times are simulated.
512 devices in a mesh: ctx: 32 (over z, core), tp: 16 (over x, y).
Axes of the slice: x: 4, y: 4, z: 16, core: 2. Of those that a mesh axis runs over, the one named last changes fastest.
Arguments:
- queries: bfloat16 [8192, 8192], P('ctx', 'tp'), may hold values from -6 to 6
- keys: bfloat16 [8192, 8192], P('ctx', 'tp'), may hold values from -0.0625 to 0.0625
- values: bfloat16 [8192, 8192], P('ctx', 'tp'), may hold values from -6 to 6
- log_keep: float32 [64, 8192], P('tp', 'ctx'), may hold values from -1 to 0, as said below
- state_in: float32 [64, 128, 128], P('tp'), may hold values from -6 to 6
- norm_gain: float32 [8192], P('tp'), may hold values from 0.1 to 1.9
- out_weight: bfloat16 [8192, 6144], P('tp', 'ctx'), may hold values from -0.125 to 0.125
Outputs:
- normed: bfloat16 [8192, 8192], P('ctx', 'tp')
- state_out: float32 [64, 128, 128], P('tp', 'ctx')
- layer_out: bfloat16 [8192, 6144], P('ctx', 'tp')
Inputs may be any that keep to these rules, and one draw needn't show every extreme that they name: `log_keep`: every entry is a logarithm of a keep factor, so at most 0.
All inputs are finite; a program needn't handle non-finite values.
Results may differ from a plain program's by a relative error of at most 0.014.
Values may be sent and summed in bfloat16 or wider, within the bound.
No kernel may reach another device: no remote copies, remote signals or barrier semaphores. Data moves between devices by JAX's collectives and lax.ppermute only.
A program may use at most 64 MiB of HBM per device.

v0:
```python
import jax
import jax.numpy as jnp
from jax import lax
from jax.sharding import Mesh, PartitionSpec as P

H = 64
DH = 128
EPSILON = 1e-06
CTX = ("za", "zb", "core")
INNER = ("zb", "core")
TP = ("x", "y")
HIGH = lax.Precision.HIGHEST
BF16 = jnp.bfloat16
F32 = jnp.float32


def split3(x):
    hi = lax.reduce_precision(x, 8, 7)
    rest = x - hi
    mid = lax.reduce_precision(rest, 8, 7)
    low = rest - mid
    return jnp.stack([hi.astype(BF16), mid.astype(BF16), low.astype(BF16)])


def join3(parts):
    parts = parts.astype(F32)
    return parts[0] + (parts[1] + parts[2])


def with_rows(block, vector):
    width = block.shape[-1]
    flat = split3(vector).reshape(-1)
    tail = jnp.pad(flat, (0, 16 * width - flat.shape[0])).reshape(16, width)
    lead = block.shape[:-2]
    tail = jnp.broadcast_to(tail, lead + tail.shape)
    return jnp.concatenate([block, tail], axis=-2)


def rows_of(tail, n):
    count = tail.shape[0]
    flat = tail.reshape(count, -1)[:, : 3 * n].reshape(count, 3, n)
    return jnp.sum(join3(jnp.moveaxis(flat, 1, 0)), axis=0)


def mixer(logs):
    count, heads = logs.shape
    upto = jnp.concatenate([jnp.zeros((1, heads), F32), jnp.cumsum(logs, axis=0)])
    before = jnp.arange(count)[None, :] < jnp.arange(count + 1)[:, None]
    gap = upto[:, None] - upto[None, 1:]
    factor = jnp.where(before[:, :, None], jnp.exp(jnp.minimum(gap, 0.0)), 0.0)
    return (upto, factor)


def per_device(queries, keys, values, log_keep, state_in, norm_gain, out_weight):
    tokens = queries.shape[0]
    heads = log_keep.shape[0]
    parts = lax.axis_size(CTX)
    quads, inner = (lax.axis_size("za"), lax.axis_size(INNER))
    rows = DH // parts
    slab = heads * quads * rows
    nx, ny = (lax.axis_size("x"), lax.axis_size("y"))
    swap = [(a * ny + b, b * ny + a) for a in range(ny) for b in range(ny)]
    moved = lax.ppermute(out_weight.T, ("zb", "y"), swap)
    gathered = lax.all_gather(moved, CTX, axis=0, tiled=True)
    cols = out_weight.shape[1] * parts // (nx * ny)
    gathered = gathered.reshape(nx, ny, cols, out_weight.shape[0])
    q = queries.reshape(tokens, heads, DH)
    k = keys.reshape(tokens, heads, DH)
    v = values.reshape(tokens, heads, DH)
    within = jnp.cumsum(log_keep, axis=1)
    own_log = within[:, -1]
    key_factor = jnp.exp(own_log[:, None] - within).T
    kdec = (k * key_factor[:, :, None]).astype(BF16)
    inc = jnp.einsum("shd,she->hde", kdec, v, preferred_element_type=F32)
    out = inc.astype(BF16).reshape(heads, quads, inner, rows, DH)
    out = out.transpose(2, 0, 1, 3, 4).reshape(inner, slab, DH)
    logs = jnp.pad(split3(own_log), ((0, 5), (0, DH - heads)))
    logs = jnp.broadcast_to(logs[None], (inner,) + logs.shape)
    got = lax.all_to_all(jnp.concatenate([out, logs], axis=1), INNER, 0, 0, tiled=True)
    causal = jnp.tril(jnp.ones((tokens, tokens), dtype=bool))
    spread = within[:, :, None] - within[:, None, :]
    decay = jnp.where(causal, jnp.exp(jnp.minimum(spread, 0.0)), 0.0)
    scores = jnp.einsum("shd,thd->hst", q, k, preferred_element_type=F32)
    weights = (scores * decay).astype(BF16)
    intra = jnp.einsum("hst,thd->shd", weights, v, preferred_element_type=F32)
    incs = got[:, :slab].astype(F32).reshape(inner, heads, -1)
    upto, mixing = mixer(join3(jnp.moveaxis(got[:, slab : slab + 3, :heads], 1, 0)))
    local = jnp.einsum("cjh,jhn->chn", mixing, incs, precision=HIGH)
    total_log = jnp.pad(upto[inner], (0, DH - heads))
    total_log = jnp.pad(total_log[None], ((0, 7), (0, 0)))
    total = jnp.concatenate([local[inner].reshape(slab, DH), total_log])
    totals = lax.all_to_all(
        jnp.broadcast_to(total[None], (quads,) + total.shape), "za", 0, 0, tiled=True
    )
    after, across = mixer(totals[:, slab, :heads])
    first = lax.dynamic_index_in_dim(
        state_in.reshape(heads, quads, inner, rows, DH), lax.axis_index(INNER), 2, keepdims=False
    ).reshape(heads, -1)
    bounds = jnp.einsum(
        "cjh,jhn->chn", across, totals[:, :slab].reshape(quads, heads, -1), precision=HIGH
    )
    bounds = bounds + jnp.exp(after)[:, :, None] * first[None]
    quad = lax.axis_index("za")
    final = lax.dynamic_index_in_dim(
        bounds[quads].reshape(heads, quads, rows, DH), quad, 1, keepdims=False
    )
    opening = lax.dynamic_index_in_dim(bounds, quad, 0, keepdims=False)
    states = local[:inner] + jnp.exp(upto[:inner])[:, :, None] * opening[None]
    states = states.astype(BF16).reshape(inner, slab, DH)
    back = lax.all_to_all(states, INNER, 0, 0, tiled=True)
    start = back.reshape(inner, heads, quads, rows, DH).transpose(1, 2, 0, 3, 4)
    start = start.reshape(heads, DH, DH)
    inter = jnp.einsum("shd,hde->she", q, start, preferred_element_type=F32)
    inter = inter * jnp.exp(within).T[:, :, None]
    attended = (intra + inter).reshape(tokens, heads * DH)
    squares = jnp.sum(attended * attended, axis=1)
    gained = attended * norm_gain
    message = with_rows(gained.astype(BF16), squares)
    message = jnp.broadcast_to(message[None], (ny,) + message.shape)
    acts = lax.all_to_all(message, "y", 0, 0, tiled=True)
    squares = rows_of(acts[:, tokens:], tokens)
    partial = jnp.stack(
        [
            sum(
                (
                    lax.dot_general(
                        acts[i, :tokens],
                        gathered[j, i],
                        (((1,), (1,)), ((), ())),
                        preferred_element_type=F32,
                    )
                    for i in range(ny)
                )
            ).astype(BF16)
            for j in range(nx)
        ]
    )
    shares = lax.all_to_all(with_rows(partial, squares), "x", 0, 0, tiled=True)
    squares = rows_of(shares[:, tokens:], tokens)
    scale = lax.rsqrt(squares / (H * DH) + EPSILON)[:, None]
    normed = (attended * scale * norm_gain).astype(BF16)
    layer_out = (jnp.sum(shares[:, :tokens].astype(F32), axis=0) * scale).astype(BF16)
    return (normed, final, layer_out)


def solution(mesh):
    fine = Mesh(mesh.devices.reshape(4, 4, 2, 4, 4), CTX + TP)
    return jax.shard_map(
        per_device,
        mesh=fine,
        in_specs=(
            P(CTX, TP),
            P(CTX, TP),
            P(CTX, TP),
            P(TP, CTX),
            P(TP, None, None),
            P(TP),
            P(TP, CTX),
        ),
        out_specs=(P(CTX, TP), P(TP, CTX, None), P(CTX, TP)),
        check_vma=False,
    )
```

profile of v0, /device:TPU:1, one launch (start us, length us, event | category | flops | bytes accessed | tf_op | source)
XLA Modules:
  0.0 151.2 jit_solution(5033377000865142325)
XLA Ops:
  7.2 1.7 %collective-permute-start = (bf16[192,512]{1,0:T(8,128)(2,1)}, bf16[192,512]{1,0:T(8,128)(2,1)S(1)}, u32[]{:S(2)}, u32[]{:S(2)}) collective-permute-start(bf16[192,512]{1,0:T(8,128)(2,1)} %bitcast.227), channel_id=1, source_target_pairs={{0,0},{1,32},{2,64},{3,96},{32,1},{33,33},{34,65},{35,97},{64,2},{... | collective-permute-start | bytes 589832 | tf_op jit(solution)/shard_map/ppermute | solution.py:63
  8.9 0.7 copy-done.2
  9.6 0.7 reshape.265
  10.3 1.2 reduce-window.6
  12.1 1.1 copy.88
  13.3 1.2 convolution_convert_fusion
  14.6 0.7 pad_maximum_fusion.2
  15.2 20.1 %all-to-all-start = ((bf16[8,72,128]{2,1,0:T(8,128)(2,1)}), bf16[8,72,128]{2,1,0:T(8,128)(2,1)S(1)}, u32[]{:S(2)}, u32[]{:S(2)}) async-start(bf16[8,72,128]{2,1,0:T(8,128)(2,1)} %pad_maximum_fusion.2), calls=%async_computation | async-start | bytes 294912 | tf_op jit(solution)/shard_map/all_to_all | solution.py:79
  35.3 6.0 %all-to-all-done = bf16[8,72,128]{2,1,0:T(8,128)(2,1)S(1)} async-done(((bf16[8,72,128]{2,1,0:T(8,128)(2,1)}), bf16[8,72,128]{2,1,0:T(8,128)(2,1)S(1)}, u32[]{:S(2)}, u32[]{:S(2)}) %all-to-all-start) | async-done | bytes 147488 | tf_op jit(solution)/shard_map/all_to_all | solution.py:79
  41.4 0.2 reduce_window_sum.47
  41.7 0.5 convolution_bitcast_fusion
  42.3 0.2 slice_reduce_fusion
  42.5 0.7 broadcast_in_dim.38
  43.1 13.7 %all-to-all-start.1 = ((f32[4,72,128]{2,1,0:T(8,128)}), f32[4,72,128]{2,1,0:T(8,128)S(1)}, u32[]{:S(2)}, u32[]{:S(2)}) async-start(f32[4,72,128]{2,1,0:T(8,128)} %broadcast_in_dim.38), calls=%async_computation.1 | async-start | bytes 294912 | tf_op jit(solution)/shard_map/all_to_all | solution.py:92
  56.9 0.8 constant_dynamic-slice_fusion.1
  57.7 17.3 %all-to-all-done.1 = f32[4,72,128]{2,1,0:T(8,128)S(1)} async-done(((f32[4,72,128]{2,1,0:T(8,128)}), f32[4,72,128]{2,1,0:T(8,128)S(1)}, u32[]{:S(2)}, u32[]{:S(2)}) %all-to-all-start.1) | async-done | bytes 147488 | tf_op jit(solution)/shard_map/all_to_all | solution.py:92
  75.4 0.5 fusion
  76.1 0.1 copy.78
  76.2 0.7 reshape.273
  77.0 4.3 %all-to-all-start.2 = ((bf16[8,64,128]{2,1,0:T(8,128)(2,1)}), bf16[8,64,128]{2,1,0:T(8,128)(2,1)S(1)}, u32[]{:S(2)}, u32[]{:S(2)}) async-start(bf16[8,64,128]{2,1,0:T(8,128)(2,1)} %reshape.273), calls=%async_computation.2 | async-start | bytes 262144 | tf_op jit(solution)/shard_map/all_to_all | solution.py:110
  81.3 0.6 convolution_bitcast_fusion.3
  81.9 5.7 %all-to-all-done.2 = bf16[8,64,128]{2,1,0:T(8,128)(2,1)S(1)} async-done(((bf16[8,64,128]{2,1,0:T(8,128)(2,1)}), bf16[8,64,128]{2,1,0:T(8,128)(2,1)S(1)}, u32[]{:S(2)}, u32[]{:S(2)}) %all-to-all-start.2) | async-done | bytes 131104 | tf_op jit(solution)/shard_map/all_to_all | solution.py:110
  87.8 0.3 multiply_reduce_fusion
  88.1 0.2 copy.84
  88.6 20.5 %all_to_all.25 = bf16[4,272,512]{2,1,0:T(8,128)(2,1)S(1)} all-to-all(bf16[4,272,512]{2,1,0:T(8,128)(2,1)S(1)} %broadcast_in_dim.40), channel_id=1, replica_groups=mesh['za'=4,'zb'=4,'core'=2,'x'=4,'y'=4] {'y'}, dimensions={0} | all-to-all | bytes 2228224 | tf_op jit(solution)/shard_map/all_to_all | solution.py:120
  109.2 4.1 %all-gather.2.cloned.1.call-done = bf16[6144,512]{1,0:T(8,128)(2,1)} async-done(((bf16[192,512]{1,0:T(8,128)(2,1)}), bf16[6144,512]{1,0:T(8,128)(2,1)}) %all-gather.2.cloned.1.call-update) | async-done | bytes 6291472 | tf_op jit(solution)/shard_map/all_gather | solution.py:64
  113.4 1.5 fusion.23
  114.8 1.7 %fusion.22 = f32[256,384]{1,0:T(8,128)S(1)} fusion(bf16[4,4,384,512]{3,2,1,0:T(8,128)(2,1)} %bitcast.189, bf16[4,272,512]{2,1,0:T(8,128)(2,1)S(1)} %all_to_all.25), kind=kOutput, calls=%fused_computation.57 | convolution fusion | flops 100663296 | bytes 1048576 | tf_op jit(solution)/shard_map/dot_general | solution.py:126
  116.5 1.3 fusion.21
  117.8 1.3 fusion.20
  119.1 1.3 convolution_add_fusion.11
  120.5 1.3 convolution_add_fusion.10
  121.8 0.3 fusion.11
  122.1 0.3 convolution_add_fusion.8
  122.4 0.3 convolution_add_fusion.7
  122.8 0.3 fusion.10
  123.1 0.3 convolution_add_fusion.5
  123.4 0.3 convolution_add_fusion.4
  123.8 0.3 fusion.9
  124.1 0.3 convolution_add_fusion.2
  124.4 0.3 convolution_add_fusion.1
  124.7 0.3 fusion.8
  125.1 1.0 pad_maximum_fusion
  126.1 4.1 %all-to-all-start.4 = ((bf16[4,272,384]{2,1,0:T(8,128)(2,1)}), bf16[4,272,384]{2,1,0:T(8,128)(2,1)S(1)}, u32[]{:S(2)}, u32[]{:S(2)}) async-start(bf16[4,272,384]{2,1,0:T(8,128)(2,1)} %pad_maximum_fusion), calls=%async_computation.4 | async-start | bytes 1671168 | tf_op jit(solution)/shard_map/all_to_all | solution.py:138
  130.2 0.6 dynamic-slice_bitcast_fusion
  130.8 11.7 %all-to-all-done.4 = bf16[4,272,384]{2,1,0:T(8,128)(2,1)S(1)} async-done(((bf16[4,272,384]{2,1,0:T(8,128)(2,1)}), bf16[4,272,384]{2,1,0:T(8,128)(2,1)S(1)}, u32[]{:S(2)}, u32[]{:S(2)}) %all-to-all-start.4) | async-done | bytes 835616 | tf_op jit(solution)/shard_map/all_to_all | solution.py:138
  142.6 0.8 multiply_convert_fusion
  143.5 0.8 multiply_convert_fusion.3
  (79 shorter events, 2.4 us)
Async XLA Ops:
  7.2 74.1 %copy-start = (bf16[256,512]{1,0:T(8,128)(2,1)S(1)}, bf16[256,512]{1,0:T(8,128)(2,1)}, u32[]{:S(2)}) copy-start(bf16[256,512]{1,0:T(8,128)(2,1)} %param.7) | copy-start | bytes 786436
  7.2 106.2 %all-gather.2.cloned.1.call-start = ((), (), s32[]{:S(2)}) async-start(), calls=%async_computation.5 | async-start | bytes 6488064 | tf_op jit(solution)/shard_map/all_gather | solution.py:64
  7.2 1.7 %collective-permute-start = (bf16[192,512]{1,0:T(8,128)(2,1)}, bf16[192,512]{1,0:T(8,128)(2,1)S(1)}, u32[]{:S(2)}, u32[]{:S(2)}) collective-permute-start(bf16[192,512]{1,0:T(8,128)(2,1)} %bitcast.227), channel_id=1, source_target_pairs={{0,0},{1,32},{2,64},{3,96},{32,1},{33,33},{34,65},{35,97},{64,2},{... | collective-permute-start | bytes 589832 | tf_op jit(solution)/shard_map/ppermute | solution.py:63
  8.9 0.7 copy-start.2
  15.2 26.1 %all-to-all-start = ((bf16[8,72,128]{2,1,0:T(8,128)(2,1)}), bf16[8,72,128]{2,1,0:T(8,128)(2,1)S(1)}, u32[]{:S(2)}, u32[]{:S(2)}) async-start(bf16[8,72,128]{2,1,0:T(8,128)(2,1)} %pad_maximum_fusion.2), calls=%async_computation | async-start | bytes 294912 | tf_op jit(solution)/shard_map/all_to_all | solution.py:79
  42.2 39.1 %copy-start.4 = (bf16[256,512]{1,0:T(8,128)(2,1)S(1)}, bf16[256,512]{1,0:T(8,128)(2,1)}, u32[]{:S(2)}) copy-start(bf16[256,512]{1,0:T(8,128)(2,1)} %param.9) | copy-start | bytes 786436
  43.1 31.9 %all-to-all-start.1 = ((f32[4,72,128]{2,1,0:T(8,128)}), f32[4,72,128]{2,1,0:T(8,128)S(1)}, u32[]{:S(2)}, u32[]{:S(2)}) async-start(f32[4,72,128]{2,1,0:T(8,128)} %broadcast_in_dim.38), calls=%async_computation.1 | async-start | bytes 294912 | tf_op jit(solution)/shard_map/all_to_all | solution.py:92
  77.0 10.6 %all-to-all-start.2 = ((bf16[8,64,128]{2,1,0:T(8,128)(2,1)}), bf16[8,64,128]{2,1,0:T(8,128)(2,1)S(1)}, u32[]{:S(2)}, u32[]{:S(2)}) async-start(bf16[8,64,128]{2,1,0:T(8,128)(2,1)} %reshape.273), calls=%async_computation.2 | async-start | bytes 262144 | tf_op jit(solution)/shard_map/all_to_all | solution.py:110
  81.9 6.5 %copy-start.3 = (f32[512]{0:T(512)S(1)}, f32[512]{0:T(512)}, u32[]{:S(2)}) copy-start(f32[512]{0:T(512)} %param.12) | copy-start | bytes 6148
  113.4 8.4 %copy-start.1 = (bf16[6144,512]{1,0:T(8,128)(2,1)S(1)}, bf16[6144,512]{1,0:T(8,128)(2,1)}, u32[]{:S(2)}) copy-start(bf16[6144,512]{1,0:T(8,128)(2,1)} %all-gather.2.cloned.1.call-done) | copy-start | bytes 18874372
  126.1 16.4 %all-to-all-start.4 = ((bf16[4,272,384]{2,1,0:T(8,128)(2,1)}), bf16[4,272,384]{2,1,0:T(8,128)(2,1)S(1)}, u32[]{:S(2)}, u32[]{:S(2)}) async-start(bf16[4,272,384]{2,1,0:T(8,128)(2,1)} %pad_maximum_fusion), calls=%async_computation.4 | async-start | bytes 1671168 | tf_op jit(solution)/shard_map/all_to_all | solution.py:138
Sparse Core Ops, SparseCore 0:
  10.7 102.6 all-gather.1
where the time goes:
time: 152 us; the launch traced here: 151 us
  waiting for transfers between devices  44.8 us (29%)
  starting transfers between devices  44 us (29%)
  blocking collectives  20.5 us (13%)
  matrix products  14.7 us (10%)
  between operations  14.5 us (10%)
  local copies, waits for them, and re-layouts  7.42 us (5%)
  other arithmetic  5.33 us (4%)
    all_to_all x1, blocking collectives, per_device(): acts = lax.all_to_all(message, 'y', 0, 0, tiled=True)  20.5 us
    all_to_all x1, starting transfers between devices, per_device(): lax.all_to_all(jnp.concatenate([out, logs], axis=1), INNER, 0, 0, tiled=T...  20.1 us
    all_to_all x1, waiting for transfers between devices, per_device(): lax.all_to_all(jnp.broadcast_to(total[None], (quads,) + total.shape), 'za...  17.3 us
    all_to_all x1, starting transfers between devices, per_device(): lax.all_to_all(jnp.broadcast_to(total[None], (quads,) + total.shape), 'za...  13.7 us
    all_to_all x1, waiting for transfers between devices, per_device(): shares = lax.all_to_all(with_rows(partial, squares), 'x', 0, 0, tiled=True)  11.7 us
    dot_general x16, matrix products, per_device(): lax.dot_general(acts[i, :tokens], gathered[j, i], (((1,), (1,)), ((), ())...  11.6 us
    all_to_all x1, waiting for transfers between devices, per_device(): lax.all_to_all(jnp.concatenate([out, logs], axis=1), INNER, 0, 0, tiled=T...  5.96 us
    all_to_all x1, waiting for transfers between devices, per_device(): back = lax.all_to_all(states, INNER, 0, 0, tiled=True)  5.68 us
  transfers between devices with their start and end apart: 6, of which 5 were waited for; matrix products, arithmetic and copies ran while one was open for 8% of the time, Pallas kernels for 0%

commit v1 on v0

--- a/solution.py
+++ b/solution.py
@@ -61,7 +61,9 @@
     nx, ny = (lax.axis_size("x"), lax.axis_size("y"))
     swap = [(a * ny + b, b * ny + a) for a in range(ny) for b in range(ny)]
     moved = lax.ppermute(out_weight.T, ("zb", "y"), swap)
-    gathered = lax.all_gather(moved, CTX, axis=0, tiled=True)
+    gathered = jnp.concatenate(
+        lax.all_to_all(jnp.stack([moved] * lax.axis_size(CTX)), CTX, 0, 0), axis=0
+    )
     cols = out_weight.shape[1] * parts // (nx * ny)
     gathered = gathered.reshape(nx, ny, cols, out_weight.shape[0])
     q = queries.reshape(tokens, heads, DH)

time: 152 us -> 420 us (2.76); the launches traced: 151 us -> 414 us
  waiting for transfers between devices: 44.8 us -> 328 us
  blocking collectives: 20.5 us -> 0 us
  between operations: 14.5 us -> 1.13 us
  matrix products: 14.7 us -> 24.1 us
    all_to_all x0 -> x2, waiting for transfers between devices: none -> 294 us  [the longest x1 274 us: per_device(): lax.all_to_all(jnp.stack([moved] * lax.axis_size(CTX)), CTX, 0, 0)]
    all_to_all x1 -> x0, blocking collectives: 20.5 us -> none  [per_device(): acts = lax.all_to_all(message, 'y', 0, 0, tiled=True)]
    all_to_all x0 -> x2, starting transfers between devices: none -> 12.6 us  [the longest x1 8.46 us: per_device(): lax.all_to_all(jnp.stack([moved] * lax.axis_size(CTX)), CTX, 0, 0)]
    all_to_all x1, starting transfers between devices: 20.1 us -> 10.1 us  [per_device(): lax.all_to_all(jnp.concatenate([out, logs], axis=1), INNER, 0, 0, tiled=T...]
    dot_general x16, matrix products: 11.6 us -> 21 us  [per_device(): lax.dot_general(acts[i, :tokens], gathered[j, i], (((1,), (1,)), ((), ())...]
    all_to_all x1, waiting for transfers between devices: 17.3 us -> 11.9 us  [per_device(): lax.all_to_all(jnp.broadcast_to(total[None], (quads,) + total.shape), 'za...]
    all_to_all x1, starting transfers between devices: 13.7 us -> 9.46 us  [per_device(): lax.all_to_all(jnp.broadcast_to(total[None], (quads,) + total.shape), 'za...]
  transfers between devices with their start and end apart: 6 -> 7, of which waited for: 5 -> 6; matrix products, arithmetic and copies ran while one was open for 8% -> 1% of each run, Pallas kernels for 0% -> 0%
where the time goes in v1:
time: 420 us; the launch traced here: 414 us
  waiting for transfers between devices  328 us (78%)
  starting transfers between devices  43.9 us (10%)
  matrix products  24.1 us (6%)
  local copies, waits for them, and re-layouts  11.1 us (3%)
  other arithmetic  5.33 us (1%)
    all_to_all x1, waiting for transfers between devices, per_device(): lax.all_to_all(jnp.stack([moved] * lax.axis_size(CTX)), CTX, 0, 0)  274 us
    dot_general x16, matrix products, per_device(): lax.dot_general(acts[i, :tokens], gathered[j, i], (((1,), (1,)), ((), ())...  21 us
    all_to_all x1, waiting for transfers between devices, per_device(): acts = lax.all_to_all(message, 'y', 0, 0, tiled=True)  19.1 us
    all_to_all x1, waiting for transfers between devices, per_device(): lax.all_to_all(jnp.broadcast_to(total[None], (quads,) + total.shape), 'za...  11.9 us
    all_to_all x1, waiting for transfers between devices, per_device(): shares = lax.all_to_all(with_rows(partial, squares), 'x', 0, 0, tiled=True)  11.5 us
    all_to_all x1, starting transfers between devices, per_device(): lax.all_to_all(jnp.concatenate([out, logs], axis=1), INNER, 0, 0, tiled=T...  10.1 us
    all_to_all x1, starting transfers between devices, per_device(): lax.all_to_all(jnp.broadcast_to(total[None], (quads,) + total.shape), 'za...  9.46 us
    all_to_all x1, starting transfers between devices, per_device(): lax.all_to_all(jnp.stack([moved] * lax.axis_size(CTX)), CTX, 0, 0)  8.46 us
  transfers between devices with their start and end apart: 7, of which 6 were waited for; matrix products, arithmetic and copies ran while one was open for 1% of the time, Pallas kernels for 0%

profile of v1, /device:TPU:1, one launch (start us, length us, event | category | flops | bytes accessed | tf_op | source)
XLA Modules:
  0.0 413.7 jit_solution(12913365220770992574)
XLA Ops:
  0.6 0.7 reshape.264
  1.4 1.2 reduce-window.6
  3.2 1.1 copy.88
  4.3 1.2 convolution_convert_fusion
  5.6 0.7 pad_maximum_fusion.2
  6.3 10.1 %all-to-all-start = ((bf16[8,72,128]{2,1,0:T(8,128)(2,1)}), bf16[8,72,128]{2,1,0:T(8,128)(2,1)S(1)}, u32[]{:S(2)}, u32[]{:S(2)}) async-start(bf16[8,72,128]{2,1,0:T(8,128)(2,1)} %pad_maximum_fusion.2), calls=%async_computation | async-start | bytes 294912 | tf_op jit(solution)/shard_map/all_to_all | solution.py:81
  16.4 6.0 %all-to-all-done = bf16[8,72,128]{2,1,0:T(8,128)(2,1)S(1)} async-done(((bf16[8,72,128]{2,1,0:T(8,128)(2,1)}), bf16[8,72,128]{2,1,0:T(8,128)(2,1)S(1)}, u32[]{:S(2)}, u32[]{:S(2)}) %all-to-all-start) | async-done | bytes 147488 | tf_op jit(solution)/shard_map/all_to_all | solution.py:81
  23.0 0.5 convolution_bitcast_fusion
  23.6 0.7 broadcast_in_dim.38
  24.2 9.5 %all-to-all-start.1 = ((f32[4,72,128]{2,1,0:T(8,128)}), f32[4,72,128]{2,1,0:T(8,128)S(1)}, u32[]{:S(2)}, u32[]{:S(2)}) async-start(f32[4,72,128]{2,1,0:T(8,128)} %broadcast_in_dim.38), calls=%async_computation.1 | async-start | bytes 294912 | tf_op jit(solution)/shard_map/all_to_all | solution.py:94
  33.7 0.8 constant_dynamic-slice_fusion.1
  34.6 11.9 %all-to-all-done.1 = f32[4,72,128]{2,1,0:T(8,128)S(1)} async-done(((f32[4,72,128]{2,1,0:T(8,128)}), f32[4,72,128]{2,1,0:T(8,128)S(1)}, u32[]{:S(2)}, u32[]{:S(2)}) %all-to-all-start.1) | async-done | bytes 147488 | tf_op jit(solution)/shard_map/all_to_all | solution.py:94
  46.8 0.5 fusion
  47.7 0.7 reshape.272
  48.4 7.0 %all-to-all-start.2 = ((bf16[8,64,128]{2,1,0:T(8,128)(2,1)}), bf16[8,64,128]{2,1,0:T(8,128)(2,1)S(1)}, u32[]{:S(2)}, u32[]{:S(2)}) async-start(bf16[8,64,128]{2,1,0:T(8,128)(2,1)} %reshape.272), calls=%async_computation.2 | async-start | bytes 262144 | tf_op jit(solution)/shard_map/all_to_all | solution.py:112
  55.5 0.6 convolution_bitcast_fusion.3
  56.1 5.1 %all-to-all-done.2 = bf16[8,64,128]{2,1,0:T(8,128)(2,1)S(1)} async-done(((bf16[8,64,128]{2,1,0:T(8,128)(2,1)}), bf16[8,64,128]{2,1,0:T(8,128)(2,1)S(1)}, u32[]{:S(2)}, u32[]{:S(2)}) %all-to-all-start.2) | async-done | bytes 131104 | tf_op jit(solution)/shard_map/all_to_all | solution.py:112
  61.4 0.3 multiply_reduce_fusion
  61.7 0.2 copy.84
  62.1 1.1 broadcast_in_dim.40
  63.2 4.2 %all-to-all-start.3 = ((bf16[4,272,512]{2,1,0:T(8,128)(2,1)}), bf16[4,272,512]{2,1,0:T(8,128)(2,1)S(1)}, u32[]{:S(2)}, u32[]{:S(2)}) async-start(bf16[4,272,512]{2,1,0:T(8,128)(2,1)} %broadcast_in_dim.40), calls=%async_computation.3 | async-start | bytes 2228224 | tf_op jit(solution)/shard_map/all_to_all | solution.py:122
  67.4 0.7 collective-permute-start
  68.1 19.1 %all-to-all-done.3 = bf16[4,272,512]{2,1,0:T(8,128)(2,1)S(1)} async-done(((bf16[4,272,512]{2,1,0:T(8,128)(2,1)}), bf16[4,272,512]{2,1,0:T(8,128)(2,1)S(1)}, u32[]{:S(2)}, u32[]{:S(2)}) %all-to-all-start.3) | async-done | bytes 1114144 | tf_op jit(solution)/shard_map/all_to_all | solution.py:122
  87.1 3.4 stack.20
  90.5 8.5 %all-to-all-start.4 = ((bf16[32,192,512]{2,1,0:T(8,128)(2,1)}), bf16[32,192,512]{2,1,0:T(8,128)(2,1)}, u32[]{:S(2)}, u32[]{:S(2)}) async-start(bf16[32,192,512]{2,1,0:T(8,128)(2,1)} %stack.20), calls=%async_computation.4 | async-start | bytes 12582912 | tf_op jit(solution)/shard_map/all_to_all | solution.py:65
  99.2 274.5 %all-to-all-done.4 = bf16[32,192,512]{2,1,0:T(8,128)(2,1)} async-done(((bf16[32,192,512]{2,1,0:T(8,128)(2,1)}), bf16[32,192,512]{2,1,0:T(8,128)(2,1)}, u32[]{:S(2)}, u32[]{:S(2)}) %all-to-all-start.4) | async-done | bytes 6291488 | tf_op jit(solution)/shard_map/all_to_all | solution.py:65
  373.7 1.3 fusion.23
  375.0 1.3 fusion.22
  376.3 1.3 fusion.21
  377.6 1.3 fusion.20
  378.9 1.3 convolution_add_fusion.11
  380.2 1.3 convolution_add_fusion.10
  381.6 1.3 fusion.11
  382.9 1.3 convolution_add_fusion.8
  384.2 1.3 convolution_add_fusion.7
  385.5 1.3 fusion.10
  386.9 1.3 convolution_add_fusion.5
  388.2 1.3 convolution_add_fusion.4
  389.5 1.3 fusion.9
  390.8 1.3 convolution_add_fusion.2
  392.1 1.3 convolution_add_fusion.1
  393.5 1.3 fusion.8
  394.8 1.0 pad_maximum_fusion
  395.8 4.0 all-to-all-start.5
  399.8 0.6 dynamic-slice_bitcast_fusion
  400.4 11.5 %all-to-all-done.5 = bf16[4,272,384]{2,1,0:T(8,128)(2,1)S(1)} async-done(((bf16[4,272,384]{2,1,0:T(8,128)(2,1)}), bf16[4,272,384]{2,1,0:T(8,128)(2,1)S(1)}, u32[]{:S(2)}, u32[]{:S(2)}) %all-to-all-start.5) | async-done | bytes 835616 | tf_op jit(solution)/shard_map/all_to_all | solution.py:140
  412.0 0.8 multiply_convert_fusion
  413.0 0.8 multiply_convert_fusion.3
  (78 shorter events, 2.8 us)
Async XLA Ops:
  0.6 54.8 %copy-start = (bf16[256,512]{1,0:T(8,128)(2,1)S(1)}, bf16[256,512]{1,0:T(8,128)(2,1)}, u32[]{:S(2)}) copy-start(bf16[256,512]{1,0:T(8,128)(2,1)} %param.7) | copy-start | bytes 786436
  6.3 16.1 %all-to-all-start = ((bf16[8,72,128]{2,1,0:T(8,128)(2,1)}), bf16[8,72,128]{2,1,0:T(8,128)(2,1)S(1)}, u32[]{:S(2)}, u32[]{:S(2)}) async-start(bf16[8,72,128]{2,1,0:T(8,128)(2,1)} %pad_maximum_fusion.2), calls=%async_computation | async-start | bytes 294912 | tf_op jit(solution)/shard_map/all_to_all | solution.py:81
  23.5 32.0 %copy-start.2 = (bf16[256,512]{1,0:T(8,128)(2,1)S(1)}, bf16[256,512]{1,0:T(8,128)(2,1)}, u32[]{:S(2)}) copy-start(bf16[256,512]{1,0:T(8,128)(2,1)} %param.9) | copy-start | bytes 786436
  24.2 22.2 %all-to-all-start.1 = ((f32[4,72,128]{2,1,0:T(8,128)}), f32[4,72,128]{2,1,0:T(8,128)S(1)}, u32[]{:S(2)}, u32[]{:S(2)}) async-start(f32[4,72,128]{2,1,0:T(8,128)} %broadcast_in_dim.38), calls=%async_computation.1 | async-start | bytes 294912 | tf_op jit(solution)/shard_map/all_to_all | solution.py:94
  48.4 12.9 %all-to-all-start.2 = ((bf16[8,64,128]{2,1,0:T(8,128)(2,1)}), bf16[8,64,128]{2,1,0:T(8,128)(2,1)S(1)}, u32[]{:S(2)}, u32[]{:S(2)}) async-start(bf16[8,64,128]{2,1,0:T(8,128)(2,1)} %reshape.272), calls=%async_computation.2 | async-start | bytes 262144 | tf_op jit(solution)/shard_map/all_to_all | solution.py:112
  56.1 5.9 %copy-start.1 = (f32[512]{0:T(512)S(1)}, f32[512]{0:T(512)}, u32[]{:S(2)}) copy-start(f32[512]{0:T(512)} %param.12) | copy-start | bytes 6148
  62.1 5.3 %copy-start.3 = (bf16[512,192]{0,1:T(8,128)(2,1)S(1)}, bf16[512,192]{0,1:T(8,128)(2,1)}, u32[]{:S(2)}) copy-start(bf16[512,192]{0,1:T(8,128)(2,1)} %param.13) | copy-start | bytes 589828
  63.2 23.9 %all-to-all-start.3 = ((bf16[4,272,512]{2,1,0:T(8,128)(2,1)}), bf16[4,272,512]{2,1,0:T(8,128)(2,1)S(1)}, u32[]{:S(2)}, u32[]{:S(2)}) async-start(bf16[4,272,512]{2,1,0:T(8,128)(2,1)} %broadcast_in_dim.40), calls=%async_computation.3 | async-start | bytes 2228224 | tf_op jit(solution)/shard_map/all_to_all | solution.py:122
  67.4 0.7 collective-permute-start
  90.5 283.2 %all-to-all-start.4 = ((bf16[32,192,512]{2,1,0:T(8,128)(2,1)}), bf16[32,192,512]{2,1,0:T(8,128)(2,1)}, u32[]{:S(2)}, u32[]{:S(2)}) async-start(bf16[32,192,512]{2,1,0:T(8,128)(2,1)} %stack.20), calls=%async_computation.4 | async-start | bytes 12582912 | tf_op jit(solution)/shard_map/all_to_all | solution.py:65
  395.8 16.2 %all-to-all-start.5 = ((bf16[4,272,384]{2,1,0:T(8,128)(2,1)}), bf16[4,272,384]{2,1,0:T(8,128)(2,1)S(1)}, u32[]{:S(2)}, u32[]{:S(2)}) async-start(bf16[4,272,384]{2,1,0:T(8,128)(2,1)} %pad_maximum_fusion), calls=%async_computation.5 | async-start | bytes 1671168 | tf_op jit(solution)/shard_map/all_to_all | solution.py:140
